TPU v7x, 128 devices: a whole 4x4x4 slice. The times are simulated.
128 devices in a mesh: tiles: 16 (over y, z), rows: 8 (over x, core).
Axes of the slice: x: 4, y: 4, z: 4, core: 2. Of those that a mesh axis runs over, the one named last changes fastest.
Arguments:
- tile_values: bfloat16 [512, 128, 128, 128], P(('tiles', 'rows')), may hold values from -6 to 6
- tile_coords: int32 [256, 3], replicated, may hold values from 0 to 127, as said below
- tile_owner: int32 [256], replicated, may hold values from 0 to 127, as said below
- factor_b: bfloat16 [16384, 128], P('rows')
- factor_c: bfloat16 [16384, 128], P('rows')
Outputs:
- factor_a: float32 [16384, 128], P('rows')
Inputs may be any that keep to these rules, and one draw needn't show every extreme that they name: `tile_owner`: devices are numbered along tiles then rows. A device holds at most 4 tiles, and in every draw some device holds exactly 4; its tiles fill its first slots in increasing order of tile number. `tile_coords`: no two tiles have the same block indices.
All inputs are finite; a program needn't handle non-finite values.
Results may differ from a plain program's by a relative error of at most 0.0003.
Values may be sent and summed in bfloat16 or wider, within the bound.
No kernel may reach another device: no remote copies, remote signals or barrier semaphores. Data moves between devices by JAX's collectives and lax.ppermute only.
A program may use at most 128 MiB of HBM per device.

v0:
```python
import jax
import jax.numpy as jnp
from jax import lax
from jax.sharding import PartitionSpec as P


def slot_table(device, tile_coords, tile_owner, slot_count):
    mine = (tile_owner == device).astype(jnp.int32)
    order = jnp.cumsum(mine) - 1
    matches = (mine[None, :] == 1) & (
        order[None, :] == jnp.arange(slot_count, dtype=jnp.int32)[:, None]
    )
    present = jnp.any(matches, axis=1)
    placed = jnp.sum(matches.astype(jnp.int32)[:, :, None] * tile_coords[None, :, :], axis=1)
    return (placed, present)


def factor_gram(block_rows):
    return lax.dot_general(
        block_rows, block_rows, (((0,), (0,)), ((), ())), preferred_element_type=jnp.float32
    )


def body(tile_values, tile_coords, tile_owner, factor_b, factor_c):
    slot_count = tile_values.shape[0]
    tile_edge = tile_values.shape[1]
    rank_width = factor_b.shape[1]
    tiles_count = lax.axis_size("tiles")
    rows_count = lax.axis_size("rows")
    tiles_index = lax.axis_index("tiles")
    rows_index = lax.axis_index("rows")
    shard_rows = factor_b.shape[0]
    owned_rows = shard_rows // tiles_count
    blocks_unit = owned_rows // tile_edge
    edge_range = jnp.arange(tile_edge, dtype=jnp.int32)
    device = tiles_index * rows_count + rows_index
    coords, present = slot_table(device, tile_coords, tile_owner, slot_count)
    need_b = (coords[:, 1][:, None] * tile_edge + edge_range[None, :]).reshape(-1)
    need_c = (coords[:, 2][:, None] * tile_edge + edge_range[None, :]).reshape(-1)
    blank = jnp.zeros((slot_count * tile_edge, rank_width), jnp.bfloat16)
    carry = (blank, blank)
    pieces = (
        lax.all_gather(factor_b, "rows", axis=0, tiled=True),
        lax.all_gather(factor_c, "rows", axis=0, tiled=True),
    )
    results = []
    for held, piece, needed in zip(carry, pieces, (need_b, need_c)):
        inside = (needed >= 0) & (needed < piece.shape[0])
        taken = jnp.take(piece, jnp.clip(needed, 0, piece.shape[0] - 1), axis=0)
        results.append(jnp.where(inside[:, None], taken, held))
    chosen_b = results[0]
    chosen_c = results[1]

    def contract(position, partials):
        tile = lax.dynamic_index_in_dim(tile_values, position, 0, keepdims=False).reshape(
            tile_edge * tile_edge, tile_edge
        )
        block_c = lax.dynamic_slice_in_dim(chosen_c, position * tile_edge, tile_edge, 0)
        block_b = lax.dynamic_slice_in_dim(chosen_b, position * tile_edge, tile_edge, 0)
        inner = jnp.dot(tile, block_c, preferred_element_type=jnp.float32).reshape(
            tile_edge, tile_edge, rank_width
        )
        contrib = jnp.sum(inner * block_b.astype(jnp.float32)[None, :, :], axis=1)
        return lax.dynamic_update_index_in_dim(partials, contrib, position, 0)

    live_count = jnp.sum(present.astype(jnp.int32))
    partials = lax.fori_loop(
        0, live_count, contract, jnp.zeros((slot_count, tile_edge, rank_width), jnp.float32)
    )
    first_blocks = coords[:, 0]
    block_rows = jnp.arange(
        lax.axis_size(("tiles", "rows")) * owned_rows // tile_edge, dtype=jnp.int32
    )
    unit_index = block_rows // blocks_unit
    offset = block_rows % blocks_unit
    global_block = (
        unit_index % rows_count * tiles_count + unit_index // rows_count
    ) * blocks_unit + offset
    one_hot = ((global_block[:, None] == first_blocks[None, :]) & present[None, :]).astype(
        jnp.float32
    )
    summed = jnp.einsum("qs,sur->qur", one_hot, partials, precision=lax.Precision.HIGHEST)
    owned_sums = lax.psum_scatter(
        summed.reshape(lax.axis_size(("tiles", "rows")) * owned_rows, rank_width),
        ("tiles", "rows"),
        scatter_dimension=0,
        tiled=True,
    )
    gram_b, gram_c = lax.psum((factor_gram(factor_b), factor_gram(factor_c)), "rows")
    normal = gram_b * gram_c
    lower = jnp.linalg.cholesky(normal)
    solved = jax.scipy.linalg.cho_solve((lower, True), owned_sums.T).T
    return lax.all_gather(solved, "tiles", axis=0, tiled=True)


def solution(mesh):
    in_specs = (P(("tiles", "rows"), None, None, None), P(), P(), P("rows", None), P("rows", None))
    out_specs = P("rows", None)
    return jax.shard_map(body, mesh=mesh, in_specs=in_specs, out_specs=out_specs, check_vma=False)
```

profile of v0, /device:TPU:0, one launch (start us, length us, event | category | flops | bytes accessed | tf_op | source)
XLA Modules:
  0.0 838.5 jit_solution(6141258442397975768)
XLA Ops:
  6.5 0.0 all-gather.6.cloned.1.call-start
  6.5 0.7 all-gather.6.cloned.1.call-update
  7.3 0.0 all-gather.4.cloned.1.call-start
  7.3 0.7 all-gather.4.cloned.1.call-update
  8.0 0.0 all-reduce.3.cloned.1.call-start
  8.1 2.2 fusion.36
  10.2 2.2 fusion.37
  12.4 0.0 all-reduce.3.cloned.1.call-update
  12.4 0.0 reduce-scatter.2.cloned.1.call-start
  12.5 0.7 fusion.33
  13.2 0.3 reduce-window.9
  13.5 0.1 slice.34
  13.6 0.1 slice_reduce_fusion
  13.7 0.1 add_bitcast_fusion
  13.8 0.1 fusion.16
  13.9 0.8 multiply_reduce_fusion.1
  14.7 0.1 fusion.22
  14.8 0.1 compare_and_fusion
  14.9 0.1 compare_select_fusion
  15.0 0.1 compare_select_fusion.1
  15.1 0.6 convert_reduce_fusion
  15.7 27.9 %all-gather.6.cloned.1.call-done = bf16[16384,128]{1,0:T(8,128)(2,1)} async-done(((bf16[2048,128]{1,0:T(8,128)(2,1)}), bf16[16384,128]{1,0:T(8,128)(2,1)}) %all-gather.6.cloned.1.call-update) | async-done | bytes 4194320 | tf_op jit(solution)/shard_map/all_gather | solution.py:43
  43.6 3.8 gather_fusion.1
  47.4 0.2 select_select_fusion
  47.6 29.8 %all-gather.4.cloned.1.call-done = bf16[16384,128]{1,0:T(8,128)(2,1)} async-done(((bf16[2048,128]{1,0:T(8,128)(2,1)}), bf16[16384,128]{1,0:T(8,128)(2,1)}) %all-gather.4.cloned.1.call-update) | async-done | bytes 4194320 | tf_op jit(solution)/shard_map/all_gather | solution.py:44
  77.4 3.8 gather_fusion
  81.2 0.2 select_select_fusion.1
  81.5 6.3 while.10
  82.1 3.4 multiply_reduce_fusion.3
  85.5 1.5 dynamic_update_slice.5
  87.8 3.6 fusion.25
  91.4 8.1 copy.21
  99.5 0.0 reduce-scatter.2.cloned.1.call-update
  99.5 0.3 all-gather.8.cloned.1.call-start
  99.7 39.3 %all-reduce.3.cloned.1.call-done = (f32[128,128]{0,1:T(8,128)}, f32[128,128]{0,1:T(8,128)}) async-done(((f32[128,128]{0,1:T(8,128)}, f32[128,128]{0,1:T(8,128)}), (f32[128,128]{0,1:T(8,128)}, f32[128,128]{0,1:T(8,128)})) %all-reduce.3.cloned.1.call-update) | async-done | bytes 131088 | tf_op jit(solution)/shard_map/psum | solution.py:89
  139.1 0.9 mul.47
  140.0 0.1 copy.19
  140.1 11.7 %cholesky.16 = f32[128,128]{1,0:T(8,128)S(1)} custom-call(f32[128,128]{1,0:T(8,128)S(1)} %fusion.13), custom_call_target="Cholesky" | custom-call | tf_op jit(solution)/shard_map/jit(cholesky)/cholesky | solution.py:91
  151.8 0.6 compare_reduce_fusion
  152.5 0.7 fusion.8
  153.1 9.8 %custom-call.10 = f32[1,128,128]{1,2,0:T(8,128)S(1)} custom-call(f32[1,128,128]{2,1,0:T(8,128)S(1)} %fusion.8), custom_call_target="InvertDiagBlocksLowerTriangular" | custom-call | tf_op jit(solution)/shard_map/jit(_cho_solve)/triangular_solve | solution.py:92
  163.0 628.2 %reduce-scatter.2.cloned.1.call-done = f32[128,128]{1,0:T(8,128)} async-done(((f32[16384,128]{1,0:T(8,128)}), f32[128,128]{1,0:T(8,128)}) %reduce-scatter.2.cloned.1.call-update) | async-done | bytes 65552 | tf_op jit(solution)/shard_map/reduce_scatter | solution.py:83
  791.2 1.1 fusion.11
  792.3 0.9 fusion.9
  793.2 0.0 all-gather.8.cloned.1.call-update
  793.3 36.5 %all-gather.8.cloned.1.call-done = f32[2048,128]{1,0:T(8,128)} async-done(((f32[128,128]{1,0:T(8,128)}), f32[2048,128]{1,0:T(8,128)}) %all-gather.8.cloned.1.call-update) | async-done | bytes 1048592 | tf_op jit(solution)/shard_map/all_gather | solution.py:93
  829.7 2.3 copy.37
  (9 shorter events, 0.2 us)
Async XLA Ops:
  6.5 37.1 %all-gather.6.cloned.1.call-start = ((), (), s32[]{:S(2)}) async-start(), calls=%async_computation.2 | async-start | bytes 4718592 | tf_op jit(solution)/shard_map/all_gather | solution.py:43
  7.3 70.2 %all-gather.4.cloned.1.call-start = ((), (), s32[]{:S(2)}) async-start(), calls=%async_computation.1 | async-start | bytes 4718592 | tf_op jit(solution)/shard_map/all_gather | solution.py:44
  8.0 131.1 %all-reduce.3.cloned.1.call-start = ((), (), s32[]{:S(2)}) async-start(), calls=%async_computation.5 | async-start | bytes 262144 | tf_op jit(solution)/shard_map/psum | solution.py:89
  12.4 778.8 %reduce-scatter.2.cloned.1.call-start = ((), (), s32[]{:S(2)}) async-start(), calls=%async_computation.3 | async-start | bytes 8454144 | tf_op jit(solution)/shard_map/reduce_scatter | solution.py:83
  99.5 730.3 %all-gather.8.cloned.1.call-start = ((), (), s32[]{:S(2)}) async-start(), calls=%async_computation.4 | async-start | bytes 1114112 | tf_op jit(solution)/shard_map/all_gather | solution.py:93
Sparse Core Ops, SparseCore 0:
  9.1 34.5 all-gather.5
  45.4 32.0 all-gather.3
  79.8 59.2 all-reduce.2
  141.4 649.7 reduce-scatter.1
  793.4 36.3 all-gather.7
where the time goes:
time: 839 us
  waiting for transfers between devices  763 us (91%)
  other arithmetic  27.2 us (3%)
  local copies, waits for them, and re-layouts  19.7 us (2%)
  matrix products  13.4 us (2%)
  between operations  13.3 us (2%)
    reduce_scatter x1, waiting for transfers between devices, body(): lax.psum_scatter(summed.reshape(lax.axis_size(('tiles', 'rows')) * owned_...  628 us
    psum x1, waiting for transfers between devices, body(): lax.psum((factor_gram(factor_b), factor_gram(factor_c)), 'rows')  39.3 us
    all_gather x1, waiting for transfers between devices, body(): return lax.all_gather(solved, 'tiles', axis=0, tiled=True)  36.5 us
    all_gather x1, waiting for transfers between devices, body(): lax.all_gather(factor_c, 'rows', axis=0, tiled=True)  29.8 us
    all_gather x1, waiting for transfers between devices, body(): lax.all_gather(factor_b, 'rows', axis=0, tiled=True)  27.9 us
  transfers between devices with their start and end apart: 5, of which 5 were waited for; matrix products, arithmetic and copies ran while one was open for 7% of the time, Pallas kernels for 0%

commit v1 on v0

--- a/solution.py
+++ b/solution.py
@@ -2,6 +2,28 @@
 import jax.numpy as jnp
 from jax import lax
 from jax.sharding import PartitionSpec as P
+
+
+def in_order(blocks, dim):
+    shape = list(blocks.shape[1:])
+    shape[dim] *= blocks.shape[0]
+    return jnp.moveaxis(blocks, 0, dim).reshape(shape)
+
+
+def gather_around(shard, axis, dim):
+    size = lax.axis_size(axis)
+    pairs = [(i, (i + 1) % size) for i in range(size)]
+    back = [(b, a) for a, b in pairs]
+    lower, upper = ([], [])
+    for hop in range(size - 1):
+        if hop % 2 == 0:
+            lower.append(lax.ppermute(lower[-1] if lower else shard, axis, pairs))
+        else:
+            upper.append(lax.ppermute(upper[-1] if upper else shard, axis, back))
+    blocks = jnp.stack([*lower[::-1], shard, *upper])
+    shift = lax.axis_index(axis) - len(lower)
+    blocks = blocks[(jnp.arange(size) - shift) % size]
+    return in_order(blocks, dim)
 
 
 def slot_table(device, tile_coords, tile_owner, slot_count):
@@ -41,7 +63,7 @@
     carry = (blank, blank)
     pieces = (
         lax.all_gather(factor_b, "rows", axis=0, tiled=True),
-        lax.all_gather(factor_c, "rows", axis=0, tiled=True),
+        gather_around(factor_c, "rows", 0),
     )
     results = []
     for held, piece, needed in zip(carry, pieces, (need_b, need_c)):

time: 839 us -> 815 us (0.971)
  waiting for transfers between devices: 763 us -> 718 us
  local copies, waits for them, and re-layouts: 19.7 us -> 31.7 us
  starting transfers between devices: 0.38 us -> 9.25 us
    ppermute x0 -> x7, waiting for transfers between devices: none -> 35.8 us  [the longest x4 35.8 us: gather_around(): lower.append(lax.ppermute(lower[-1] if lower else shard, axis, pairs))]
    all_gather x1 -> x0, waiting for transfers between devices: 29.8 us -> none  [body(): lax.all_gather(factor_c, 'rows', axis=0, tiled=True)]
    all_gather x1, waiting for transfers between devices: 27.9 us -> 0.02 us  [body(): lax.all_gather(factor_b, 'rows', axis=0, tiled=True)]
    psum x1, waiting for transfers between devices: 39.3 us -> 13.4 us  [body(): lax.psum((factor_gram(factor_b), factor_gram(factor_c)), 'rows')]
    ppermute x0 -> x7, starting transfers between devices: none -> 8.91 us  [the longest x3 8.87 us: gather_around(): upper.append(lax.ppermute(upper[-1] if upper else shard, axis, back))]
  transfers between devices with their start and end apart: 5 -> 11, of which waited for: 5 -> 6; matrix products, arithmetic and copies ran while one was open for 7% -> 8% of each run, Pallas kernels for 0% -> 0%
where the time goes in v1:
time: 815 us; the launch traced here: 814 us
  waiting for transfers between devices  718 us (88%)
  local copies, waits for them, and re-layouts  31.7 us (4%)
  other arithmetic  27.2 us (3%)
  matrix products  13.5 us (2%)
  between operations  13.3 us (2%)
  starting transfers between devices  9.25 us (1%)
    reduce_scatter x1, waiting for transfers between devices, body(): lax.psum_scatter(summed.reshape(lax.axis_size(('tiles', 'rows')) * owned_...  631 us
    all_gather x1, waiting for transfers between devices, body(): return lax.all_gather(solved, 'tiles', axis=0, tiled=True)  37.5 us
    ppermute x4, waiting for transfers between devices, gather_around(): lower.append(lax.ppermute(lower[-1] if lower else shard, axis, pairs))  35.8 us
  transfers between devices with their start and end apart: 11, of which 6 were waited for; matrix products, arithmetic and copies ran while one was open for 8% of the time, Pallas kernels for 0%

profile of v1, /device:TPU:0, one launch (start us, length us, event | category | flops | bytes accessed | tf_op | source)
XLA Modules:
  0.0 814.5 jit_solution(18086778962422345229)
XLA Ops:
  6.5 0.7 all-gather.3.cloned.1.call-update
  7.3 0.0 all-reduce.3.cloned.1.call-start
  7.3 0.0 collective-permute-start
  7.3 2.9 collective-permute-start.4
  10.3 2.2 fusion.38
  12.4 2.2 fusion.39
  14.6 0.0 all-reduce.3.cloned.1.call-update
  14.7 0.0 reduce-scatter.2.cloned.1.call-start
  14.7 0.7 fusion.33
  15.4 0.3 reduce-window.9
  15.7 0.1 slice.34
  15.8 0.1 slice_reduce_fusion
  16.0 0.1 add_bitcast_fusion
  16.0 0.1 fusion.16
  16.2 0.6 convert_reduce_fusion
  16.8 0.8 multiply_reduce_fusion.1
  17.6 0.0 collective-permute-done
  17.6 0.0 collective-permute-start.1
  17.7 0.1 compare_select_fusion.1
  17.8 14.2 %collective-permute-done.1 = bf16[2048,128]{1,0:T(8,128)(2,1)S(1)} collective-permute-done((bf16[2048,128]{1,0:T(8,128)(2,1)S(1)}, bf16[2048,128]{1,0:T(8,128)(2,1)S(1)}, u32[]{:S(2)}, u32[]{:S(2)}) %collective-permute-start.1) | collective-permute-done | bytes 524320 | tf_op jit(solution)/shard_map/ppermute | solution.py:20
  32.0 0.0 collective-permute-start.2
  32.0 0.1 compare_select_fusion
  32.1 3.0 collective-permute-start.5
  35.1 14.9 %collective-permute-done.2 = bf16[2048,128]{1,0:T(8,128)(2,1)S(1)} collective-permute-done((bf16[2048,128]{1,0:T(8,128)(2,1)S(1)}, bf16[2048,128]{1,0:T(8,128)(2,1)S(1)}, u32[]{:S(2)}, u32[]{:S(2)}) %collective-permute-start.2) | collective-permute-done | bytes 524320 | tf_op jit(solution)/shard_map/ppermute | solution.py:20
  49.9 0.0 collective-permute-start.3
  49.9 0.1 fusion.22
  50.0 0.1 compare_and_fusion
  50.1 0.0 collective-permute-done.5
  50.1 3.0 collective-permute-start.6
  53.1 6.7 collective-permute-done.3
  59.8 0.8 bitcast_dynamic-update-slice_fusion.7
  60.6 0.9 bitcast_dynamic-update-slice_fusion.6
  61.4 0.8 bitcast_dynamic-update-slice_fusion.5
  62.3 0.8 bitcast_dynamic-update-slice_fusion.4
  63.1 0.8 bitcast_dynamic-update-slice_fusion.3
  64.0 0.9 bitcast_dynamic-update-slice_fusion.2
  64.8 0.8 bitcast_dynamic-update-slice_fusion.1
  65.6 0.8 bitcast_dynamic-update-slice_fusion
  66.5 5.3 gather_fusion
  71.7 3.8 gather_fusion.1
  75.5 0.2 select_select_fusion.1
  75.8 0.0 all-gather.3.cloned.1.call-done
  75.8 3.8 gather_fusion.2
  79.6 0.2 select_select_fusion
  79.8 6.4 while.10
  80.5 3.5 multiply_reduce_fusion.3
  84.0 1.5 dynamic_update_slice.5
  86.3 3.6 fusion.25
  89.9 8.1 copy.21
  97.9 0.0 reduce-scatter.2.cloned.1.call-update
  98.0 0.3 all-gather.5.cloned.1.call-start
  98.2 13.4 %all-reduce.3.cloned.1.call-done = (f32[128,128]{0,1:T(8,128)}, f32[128,128]{0,1:T(8,128)}) async-done(((f32[128,128]{0,1:T(8,128)}, f32[128,128]{0,1:T(8,128)}), (f32[128,128]{0,1:T(8,128)}, f32[128,128]{0,1:T(8,128)})) %all-reduce.3.cloned.1.call-update) | async-done | bytes 131088 | tf_op jit(solution)/shard_map/psum | solution.py:111
  111.6 0.9 mul.47
  112.5 0.1 copy.19
  112.6 11.7 %cholesky.16 = f32[128,128]{1,0:T(8,128)S(1)} custom-call(f32[128,128]{1,0:T(8,128)S(1)} %fusion.13), custom_call_target="Cholesky" | custom-call | tf_op jit(solution)/shard_map/jit(cholesky)/cholesky | solution.py:113
  124.3 0.6 compare_reduce_fusion
  125.0 0.7 fusion.8
  125.7 9.8 %custom-call.10 = f32[1,128,128]{1,2,0:T(8,128)S(1)} custom-call(f32[1,128,128]{2,1,0:T(8,128)S(1)} %fusion.8), custom_call_target="InvertDiagBlocksLowerTriangular" | custom-call | tf_op jit(solution)/shard_map/jit(_cho_solve)/triangular_solve | solution.py:114
  135.5 630.6 %reduce-scatter.2.cloned.1.call-done = f32[128,128]{1,0:T(8,128)} async-done(((f32[16384,128]{1,0:T(8,128)}), f32[128,128]{1,0:T(8,128)}) %reduce-scatter.2.cloned.1.call-update) | async-done | bytes 65552 | tf_op jit(solution)/shard_map/reduce_scatter | solution.py:105
  766.1 1.1 fusion.11
  767.2 0.9 fusion.9
  768.1 0.0 all-gather.5.cloned.1.call-update
  768.1 37.5 %all-gather.5.cloned.1.call-done = f32[2048,128]{1,0:T(8,128)} async-done(((f32[128,128]{1,0:T(8,128)}), f32[2048,128]{1,0:T(8,128)}) %all-gather.5.cloned.1.call-update) | async-done | bytes 1048592 | tf_op jit(solution)/shard_map/all_gather | solution.py:115
  805.7 2.3 copy.44
  (16 shorter events, 0.2 us)
Async XLA Ops:
  6.5 56.6 %copy-start = (bf16[2048,128]{1,0:T(8,128)(2,1)S(1)}, bf16[2048,128]{1,0:T(8,128)(2,1)}, u32[]{:S(2)}) copy-start(bf16[2048,128]{1,0:T(8,128)(2,1)} %param.13) | copy-start | bytes 1572868
  6.5 69.2 %all-gather.3.cloned.1.call-start = ((), (), s32[]{:S(2)}) async-start(), calls=%async_computation.1 | async-start | bytes 4718592 | tf_op jit(solution)/shard_map/all_gather | solution.py:65
  7.3 104.3 %all-reduce.3.cloned.1.call-start = ((), (), s32[]{:S(2)}) async-start(), calls=%async_computation.4 | async-start | bytes 262144 | tf_op jit(solution)/shard_map/psum | solution.py:111
  7.3 10.3 %collective-permute-start = (bf16[2048,128]{1,0:T(8,128)(2,1)}, bf16[2048,128]{1,0:T(8,128)(2,1)S(1)}, u32[]{:S(2)}, u32[]{:S(2)}) collective-permute-start(bf16[2048,128]{1,0:T(8,128)(2,1)} %param.13), channel_id=1, source_target_pairs={{0,1},{1,2},{2,3},{3,4},{4,5},{5,6},{6,7},{7,0},{8,9},{9,10},{10,1... | collective-permute-start | bytes 1572872 | tf_op jit(solution)/shard_map/ppermute | solution.py:20
  7.3 24.8 %collective-permute-start.4 = (bf16[2048,128]{1,0:T(8,128)(2,1)}, bf16[2048,128]{1,0:T(8,128)(2,1)S(1)}, u32[]{:S(2)}, u32[]{:S(2)}) collective-permute-start(bf16[2048,128]{1,0:T(8,128)(2,1)} %param.13), channel_id=1, source_target_pairs={{1,0},{2,1},{3,2},{4,3},{5,4},{6,5},{7,6},{0,7},{9,8},{10,9},{11,1... | collective-permute-start | bytes 1572872 | tf_op jit(solution)/shard_map/ppermute | solution.py:22
  14.7 751.4 %reduce-scatter.2.cloned.1.call-start = ((), (), s32[]{:S(2)}) async-start(), calls=%async_computation.2 | async-start | bytes 8454144 | tf_op jit(solution)/shard_map/reduce_scatter | solution.py:105
  17.6 14.4 %collective-permute-start.1 = (bf16[2048,128]{1,0:T(8,128)(2,1)S(1)}, bf16[2048,128]{1,0:T(8,128)(2,1)S(1)}, u32[]{:S(2)}, u32[]{:S(2)}) collective-permute-start(bf16[2048,128]{1,0:T(8,128)(2,1)S(1)} %collective-permute-done), channel_id=1, source_target_pairs={{0,1},{1,2},{2,3},{3,4},{4,5},{5,6},{6,7},{7,0},{8,9},{9,10},{10,1... | collective-permute-start | bytes 1572872 | tf_op jit(solution)/shard_map/ppermute | solution.py:20
  32.0 17.9 %collective-permute-start.2 = (bf16[2048,128]{1,0:T(8,128)(2,1)S(1)}, bf16[2048,128]{1,0:T(8,128)(2,1)S(1)}, u32[]{:S(2)}, u32[]{:S(2)}) collective-permute-start(bf16[2048,128]{1,0:T(8,128)(2,1)S(1)} %collective-permute-done.1), channel_id=1, source_target_pairs={{0,1},{1,2},{2,3},{3,4},{4,5},{5,6},{6,7},{7,0},{8,9},{9,10},{10,1... | collective-permute-start | bytes 1572872 | tf_op jit(solution)/shard_map/ppermute | solution.py:20
  32.1 18.0 %collective-permute-start.5 = (bf16[2048,128]{1,0:T(8,128)(2,1)S(1)}, bf16[2048,128]{1,0:T(8,128)(2,1)S(1)}, u32[]{:S(2)}, u32[]{:S(2)}) collective-permute-start(bf16[2048,128]{1,0:T(8,128)(2,1)S(1)} %collective-permute-done.4), channel_id=1, source_target_pairs={{1,0},{2,1},{3,2},{4,3},{5,4},{6,5},{7,6},{0,7},{9,8},{10,9},{11,1... | collective-permute-start | bytes 1572872 | tf_op jit(solution)/shard_map/ppermute | solution.py:22
  49.9 9.8 %collective-permute-start.3 = (bf16[2048,128]{1,0:T(8,128)(2,1)S(1)}, bf16[2048,128]{1,0:T(8,128)(2,1)S(1)}, u32[]{:S(2)}, u32[]{:S(2)}) collective-permute-start(bf16[2048,128]{1,0:T(8,128)(2,1)S(1)} %collective-permute-done.2), channel_id=1, source_target_pairs={{0,1},{1,2},{2,3},{3,4},{4,5},{5,6},{6,7},{7,0},{8,9},{9,10},{10,1... | collective-permute-start | bytes 1572872 | tf_op jit(solution)/shard_map/ppermute | solution.py:20
  50.1 15.5 %collective-permute-start.6 = (bf16[2048,128]{1,0:T(8,128)(2,1)S(1)}, bf16[2048,128]{1,0:T(8,128)(2,1)S(1)}, u32[]{:S(2)}, u32[]{:S(2)}) collective-permute-start(bf16[2048,128]{1,0:T(8,128)(2,1)S(1)} %collective-permute-done.5), channel_id=1, source_target_pairs={{1,0},{2,1},{3,2},{4,3},{5,4},{6,5},{7,6},{0,7},{9,8},{10,9},{11,1... | collective-permute-start | bytes 1572872 | tf_op jit(solution)/shard_map/ppermute | solution.py:22
  98.0 707.7 %all-gather.5.cloned.1.call-start = ((), (), s32[]{:S(2)}) async-start(), calls=%async_computation.3 | async-start | bytes 1114112 | tf_op jit(solution)/shard_map/all_gather | solution.py:115
Sparse Core Ops, SparseCore 0:
  9.1 40.9 all-gather.2
  52.4 59.1 all-reduce.2
  114.1 651.9 reduce-scatter.1
  768.2 37.3 all-gather.4
